TPU v7x, 32 devices: a whole 2x2x4 slice. The times are simulated.
32 devices in a mesh: head: 4 (over y, x), seq: 8 (over z, core).
Axes of the slice: x: 2, y: 2, z: 4, core: 2. Of those that a mesh axis runs over, the one named last changes fastest.
Arguments:
- queries: bfloat16 [8, 64, 576], P('seq', 'head'), may hold values from -400 to 400
- query_pos: int32 [8], replicated, may hold values from 2019 to 2047, as said below
- latents: bfloat16 [2048, 576], P('seq'), may hold values from -6 to 6
- valid_keys: int32 [8], P('seq'), may hold values from 128 to 256, as said below
- output_gradient: bfloat16 [8, 64, 512], P('seq', 'head'), may hold values from -600 to 600
- kv_down: bfloat16 [7168, 576], P('head'), may hold values from -0.0625 to 0.0625
Outputs:
- latent_grad: float32 [2048, 576], P('seq')
- input_grad: bfloat16 [2048, 7168], P('seq', 'head')
Inputs may be any that keep to these rules, and one draw needn't show every extreme that they name: `query_pos`: positions rise strictly with the query index, consecutive ones differ by 1 to 4, and the last is 2047. The first valid_keys[s] positions of shard s are valid; some shard is full and some holds exactly half.
All inputs are finite; a program needn't handle non-finite values.
Results may differ from a plain program's by a relative error of at most 0.015.
Values may be sent and summed in bfloat16 or wider, within the bound.
No kernel may reach another device: no remote copies, remote signals or barrier semaphores. Data moves between devices by JAX's collectives and lax.ppermute only.
A program may use at most 64 MiB of HBM per device.

v0:
```python
import jax
import jax.numpy as jnp
from jax import lax
from jax.sharding import PartitionSpec as P

score_scale = 192.0 ** (-0.5)


def combined_all(value, axis, join):
    pieces = jax.tree.map(lambda part: lax.all_gather(part, axis), value)
    head = jax.tree.map(lambda part: part[0], pieces)
    tail = jax.tree.map(lambda part: part[1:], pieces)
    so_far, _ = lax.scan(lambda so_far, share: (join(so_far, share), None), head, tail)
    return so_far


def join_totals(first_part, second_part):
    top = jnp.maximum(first_part[0], second_part[0])
    first_weight = jnp.exp(first_part[0] - top)
    second_weight = jnp.exp(second_part[0] - top)
    return (top, first_part[1] * first_weight + second_part[1] * second_weight)


def shards(queries, query_pos, latents, valid_keys, output_gradient, kv_down):
    key_count = latents.shape[0]
    latent_span = output_gradient.shape[2]
    all_query, gradient_total = (
        lax.all_gather(queries, "seq", axis=0, tiled=True),
        lax.all_gather(output_gradient, "seq", axis=0, tiled=True),
    )
    first_key = lax.axis_index("seq") * key_count
    local_index = jnp.arange(key_count, dtype=jnp.int32)
    key_pos = first_key + local_index
    visible = (local_index < valid_keys[0])[None, :] & (key_pos[None, :] <= query_pos[:, None])
    visible = visible[:, None, :]
    scores = (
        jnp.einsum("qhc,kc->qhk", all_query, latents, preferred_element_type=jnp.float32)
        * score_scale
    )
    scores = jnp.where(visible, scores, -1e30)
    local_max = jnp.max(scores, axis=-1)
    shifted = jnp.where(visible, jnp.exp(scores - local_max[..., None]), 0.0)
    local_total = jnp.sum(shifted, axis=-1)
    dprobs = jnp.einsum(
        "mcg,dg->mcd", gradient_total, latents[:, :latent_span], preferred_element_type=jnp.float32
    )
    row_max, row_total = combined_all((local_max, local_total), "seq", join_totals)
    lse = row_max + jnp.log(row_total)
    probs = jnp.where(visible, jnp.exp(scores - lse[..., None]), 0.0)
    delta_rows = lax.psum(jnp.sum(probs * dprobs, axis=-1), "seq")
    dscores = probs * (dprobs - delta_rows[..., None])
    probs_b = probs.astype(jnp.bfloat16)
    dscores_b = dscores.astype(jnp.bfloat16)
    key_contribution = (
        jnp.einsum("qhk,qhc->kc", dscores_b, all_query, preferred_element_type=jnp.float32)
        * score_scale
    )
    value_contribution = jnp.einsum(
        "qhk,qhv->kv", probs_b, gradient_total, preferred_element_type=jnp.float32
    )
    owned = lax.psum_scatter(
        jnp.concatenate(
            [
                key_contribution[:, :latent_span] + value_contribution,
                key_contribution[:, latent_span:],
            ],
            axis=1,
        ).astype(jnp.bfloat16),
        "head",
        scatter_dimension=0,
        tiled=True,
    ).astype(jnp.float32)
    latent_grad = lax.all_gather(owned.astype(jnp.bfloat16), "head", axis=0, tiled=True).astype(
        owned.dtype
    )
    input_grad = lax.dot_general(
        latent_grad.astype(jnp.bfloat16),
        kv_down,
        (((1,), (1,)), ((), ())),
        preferred_element_type=jnp.float32,
    ).astype(jnp.bfloat16)
    return (latent_grad, input_grad)


def solution(mesh):
    placed = (
        P("seq", "head", None),
        P(),
        P("seq", None),
        P("seq"),
        P("seq", "head", None),
        P("head", None),
    )
    return jax.shard_map(
        shards,
        mesh=mesh,
        in_specs=placed,
        out_specs=(P("seq", None), P("seq", "head")),
        check_vma=False,
    )
```

profile of v0, /device:TPU:0, one launch (start us, length us, event | category | flops | bytes accessed | tf_op | source)
XLA Modules:
  0.0 130.2 jit_solution(3458385779859424649)
XLA Ops:
  7.2 0.0 copy-start
  7.2 0.0 reduce-scatter.4.cloned.1.call-start
  8.0 15.9 %all_gather.21 = bf16[8,16,576]{2,1,0:T(8,128)(2,1)S(1)} all-gather(bf16[1,16,576]{2,1,0:T(8,128)(2,1)} %param.8), channel_id=1, replica_groups=mesh['head'=4,'seq'=8] {'seq'}, dimensions={0}, use_global_device_ids=true | all-gather | bytes 165888 | tf_op jit(solution)/shard_map/all_gather | solution.py:28
  24.0 0.7 compare_and_fusion
  24.7 1.2 fusion.21
  26.0 14.1 %all-gather = f32[64,16]{1,0:T(8,128)S(1)} all-gather(f32[8,16]{1,0:T(8,128)S(1)} %get-tuple-element.46), channel_id=2, replica_groups=mesh['head'=4,'seq'=8] {'seq'}, dimensions={0}, use_global_device_ids=true | all-gather | bytes 4608 | tf_op jit(solution)/shard_map/all_gather | solution.py:10
  40.1 0.2 select_reduce_fusion
  40.2 14.1 %all-gather.1 = f32[64,16]{1,0:T(8,128)S(1)} all-gather(f32[8,16]{1,0:T(8,128)S(1)} %select_reduce_fusion), channel_id=3, replica_groups=mesh['head'=4,'seq'=8] {'seq'}, dimensions={0}, use_global_device_ids=true | all-gather | bytes 4608 | tf_op jit(solution)/shard_map/all_gather | solution.py:10
  54.3 14.2 %all_gather.26 = bf16[8,16,512]{2,1,0:T(8,128)(2,1)S(1)} all-gather(bf16[1,16,512]{2,1,0:T(8,128)(2,1)} %param.12), channel_id=1, replica_groups=mesh['head'=4,'seq'=8] {'seq'}, dimensions={0}, use_global_device_ids=true | all-gather | bytes 147456 | tf_op jit(solution)/shard_map/all_gather | solution.py:29
  68.5 0.2 while.12
  68.8 1.2 multiply_reduce_fusion
  70.0 16.9 %psum.7 = f32[8,16]{1,0:T(8,128)S(1)} all-reduce(f32[8,16]{1,0:T(8,128)S(1)} %get-tuple-element.48), channel_id=1, replica_groups=mesh['head'=4,'seq'=8] {'seq'}, use_global_device_ids=true, to_apply=%region_5.6 | all-reduce | flops 128 | bytes 1024 | tf_op jit(solution)/shard_map/psum | solution.py:50
  86.9 0.3 fusion.2
  87.2 0.3 fusion.4
  87.6 0.9 copy.16
  88.5 0.0 reduce-scatter.4.cloned.1.call-update
  88.5 22.9 %reduce-scatter.4.cloned.1.call-done = bf16[64,576]{1,0:T(8,128)(2,1)} async-done(((bf16[256,576]{1,0:T(8,128)(2,1)}), bf16[64,576]{1,0:T(8,128)(2,1)}) %reduce-scatter.4.cloned.1.call-update) | async-done | bytes 73744 | tf_op jit(solution)/shard_map/reduce_scatter | solution.py:61
  111.4 9.2 %all_gather.27 = bf16[256,576]{1,0:T(8,128)(2,1)S(1)} all-gather(bf16[64,576]{1,0:T(8,128)(2,1)} %reduce-scatter.4.cloned.1.call-done), channel_id=1, replica_groups=mesh['head'=4,'seq'=8] {'head'}, dimensions={0}, use_global_device_ids=true | all-gather | bytes 368640 | tf_op jit(solution)/shard_map/all_gather | solution.py:73
  120.6 1.0 copy.13
  121.6 0.0 copy-done
  121.6 1.8 %convolution_convert_fusion = bf16[256,1792]{1,0:T(8,128)(2,1)} fusion(bf16[256,576]{1,0:T(8,128)(2,1)S(1)} %all_gather.27, bf16[1792,576]{0,1:T(8,128)(2,1)S(1)} %copy-done), kind=kOutput, calls=%fused_computation.5 | convolution fusion | flops 528941056 | bytes 3276800 | tf_op jit(solution)/shard_map/dot_general | solution.py:76
  (16 shorter events, 0.2 us)
Async XLA Ops:
  7.2 114.4 %copy-start = (bf16[1792,576]{0,1:T(8,128)(2,1)S(1)}, bf16[1792,576]{0,1:T(8,128)(2,1)}, u32[]{:S(2)}) copy-start(bf16[1792,576]{0,1:T(8,128)(2,1)} %param.13) | copy-start | bytes 6193156
  7.2 104.2 %reduce-scatter.4.cloned.1.call-start = ((), (), s32[]{:S(2)}) async-start(), calls=%async_computation.1 | async-start | bytes 409600 | tf_op jit(solution)/shard_map/reduce_scatter | solution.py:61
Sparse Core Ops, SparseCore 0:
  88.6 22.7 reduce-scatter.3
where the time goes:
time: 131 us; the launch traced here: 130 us
  blocking collectives  84.4 us (64%)
  waiting for transfers between devices  22.9 us (17%)
  between operations  14.9 us (11%)
  matrix products  4.91 us (4%)
  local copies, waits for them, and re-layouts  1.9 us (1%)
    all_gather x2, blocking collectives, combined_all(): pieces = jax.tree.map(lambda part: lax.all_gather(part, axis), value)  28.2 us
    reduce_scatter x1, waiting for transfers between devices, shards(): lax.psum_scatter(jnp.concatenate([key_contribution[:, :latent_span] + val...  22.9 us
    psum x1, blocking collectives, shards(): delta_rows = lax.psum(jnp.sum(probs * dprobs, axis=-1), 'seq')  16.9 us
    all_gather x1, blocking collectives, shards(): lax.all_gather(queries, 'seq', axis=0, tiled=True)  15.9 us
    all_gather x1, blocking collectives, shards(): lax.all_gather(output_gradient, 'seq', axis=0, tiled=True)  14.2 us
    all_gather x1, blocking collectives, shards(): lax.all_gather(owned.astype(jnp.bfloat16), 'head', axis=0, tiled=True)  9.19 us
  transfers between devices with their start and end apart: 1, of which 1 were waited for; matrix products, arithmetic and copies ran while one was open for 0% of the time, Pallas kernels for 0%

commit v1 on v0

--- a/solution.py
+++ b/solution.py
@@ -25,7 +25,9 @@
     key_count = latents.shape[0]
     latent_span = output_gradient.shape[2]
     all_query, gradient_total = (
-        lax.all_gather(queries, "seq", axis=0, tiled=True),
+        jnp.concatenate(
+            lax.all_to_all(jnp.stack([queries] * lax.axis_size("seq")), "seq", 0, 0), axis=0
+        ),
         lax.all_gather(output_gradient, "seq", axis=0, tiled=True),
     )
     first_key = lax.axis_index("seq") * key_count

time: 131 us -> 123 us (0.939)
  blocking collectives: 84.4 us -> 68.8 us
  starting transfers between devices: 0.04 us -> 6.39 us
  local copies, waits for them, and re-layouts: 1.9 us -> 3.46 us
    all_gather x1 -> x0, blocking collectives: 15.9 us -> none  [shards(): lax.all_gather(queries, 'seq', axis=0, tiled=True)]
    all_to_all x0 -> x1, starting transfers between devices: none -> 6.35 us  [shards(): lax.all_to_all(jnp.stack([queries] * lax.axis_size('seq')), 'seq', 0, 0)]
    another operation x0 -> x1, local copies, waits for them, and re-layouts: none -> 1.55 us  [shards(): jnp.stack([queries] * lax.axis_size('seq'))]
  transfers between devices with their start and end apart: 1 -> 2, of which waited for: 1 -> 1; matrix products, arithmetic and copies ran while one was open for 0% -> 1% of each run, Pallas kernels for 0% -> 0%
where the time goes in v1:
time: 123 us; the launch traced here: 122 us
  blocking collectives  68.8 us (56%)
  waiting for transfers between devices  22.9 us (19%)
  between operations  14.8 us (12%)
  starting transfers between devices  6.39 us (5%)
  matrix products  4.9 us (4%)
  local copies, waits for them, and re-layouts  3.46 us (3%)
    all_gather x2, blocking collectives, combined_all(): pieces = jax.tree.map(lambda part: lax.all_gather(part, axis), value)  28.2 us
    reduce_scatter x1, waiting for transfers between devices, shards(): lax.psum_scatter(jnp.concatenate([key_contribution[:, :latent_span] + val...  22.9 us
    psum x1, blocking collectives, shards(): delta_rows = lax.psum(jnp.sum(probs * dprobs, axis=-1), 'seq')  16.4 us
    all_gather x1, blocking collectives, shards(): lax.all_gather(output_gradient, 'seq', axis=0, tiled=True)  15 us
    all_gather x1, blocking collectives, shards(): lax.all_gather(owned.astype(jnp.bfloat16), 'head', axis=0, tiled=True)  9.18 us
    all_to_all x1, starting transfers between devices, shards(): lax.all_to_all(jnp.stack([queries] * lax.axis_size('seq')), 'seq', 0, 0)  6.35 us
  transfers between devices with their start and end apart: 2, of which 1 were waited for; matrix products, arithmetic and copies ran while one was open for 1% of the time, Pallas kernels for 0%

profile of v1, /device:TPU:0, one launch (start us, length us, event | category | flops | bytes accessed | tf_op | source)
XLA Modules:
  0.0 122.4 jit_solution(11645397014605072411)
XLA Ops:
  7.2 0.0 copy-start
  7.2 1.6 %stack.2 = bf16[8,1,16,576]{3,2,1,0:T(8,128)(2,1)} broadcast(bf16[16,576]{1,0:T(8,128)(2,1)} %bitcast.54), dimensions={2,3} | broadcast | bytes 165888 | tf_op jit(solution)/shard_map/stack | solution.py:29
  8.7 6.4 %all-to-all-start = ((bf16[8,1,16,576]{3,2,1,0:T(8,128)(2,1)}), bf16[8,1,16,576]{3,2,1,0:T(8,128)(2,1)S(1)}, u32[]{:S(2)}, u32[]{:S(2)}) async-start(bf16[8,1,16,576]{3,2,1,0:T(8,128)(2,1)} %stack.2), calls=%async_computation | async-start | bytes 327680 | tf_op jit(solution)/shard_map/all_to_all | solution.py:29
  15.1 0.0 reduce-scatter.4.cloned.1.call-start
  15.8 15.0 %all_gather.22 = bf16[8,16,512]{2,1,0:T(8,128)(2,1)S(1)} all-gather(bf16[1,16,512]{2,1,0:T(8,128)(2,1)} %param.12), channel_id=1, replica_groups=mesh['head'=4,'seq'=8] {'seq'}, dimensions={0}, use_global_device_ids=true | all-gather | bytes 147456 | tf_op jit(solution)/shard_map/all_gather | solution.py:31
  30.8 0.7 compare_and_fusion
  31.6 0.0 all-to-all-done
  31.6 1.2 %fusion.23 = (f32[8,16]{1,0:T(8,128)S(1)}, f32[8,16,256]{2,1,0:T(8,128)S(1)}) fusion(bf16[256,576]{0,1:T(8,128)(2,1)} %param.10, bf16[8,1,16,576]{3,2,1,0:T(8,128)(2,1)S(1)} %all-to-all-done, pred[8,256]{1,0:T(8,128)(4,1)S(1)} %compare_and_fusion), kind=kOutput, calls=%fused_computation.41 | convolution fusion | flops 37846912 | bytes 576000 | tf_op jit(solution)/shard_map/qhc,kc->qhk/dot_general | solution.py:39
  32.8 14.1 %all-gather = f32[64,16]{1,0:T(8,128)S(1)} all-gather(f32[8,16]{1,0:T(8,128)S(1)} %get-tuple-element.46), channel_id=2, replica_groups=mesh['head'=4,'seq'=8] {'seq'}, dimensions={0}, use_global_device_ids=true | all-gather | bytes 4608 | tf_op jit(solution)/shard_map/all_gather | solution.py:10
  46.9 0.2 select_reduce_fusion
  47.1 14.1 %all-gather.1 = f32[64,16]{1,0:T(8,128)S(1)} all-gather(f32[8,16]{1,0:T(8,128)S(1)} %select_reduce_fusion), channel_id=3, replica_groups=mesh['head'=4,'seq'=8] {'seq'}, dimensions={0}, use_global_device_ids=true | all-gather | bytes 4608 | tf_op jit(solution)/shard_map/all_gather | solution.py:10
  61.2 0.2 while.12
  61.5 1.2 multiply_reduce_fusion
  62.7 16.4 %psum.7 = f32[8,16]{1,0:T(8,128)S(1)} all-reduce(f32[8,16]{1,0:T(8,128)S(1)} %get-tuple-element.48), channel_id=1, replica_groups=mesh['head'=4,'seq'=8] {'seq'}, use_global_device_ids=true, to_apply=%region_5.6 | all-reduce | flops 128 | bytes 1024 | tf_op jit(solution)/shard_map/psum | solution.py:52
  79.1 0.3 fusion.2
  79.5 0.3 fusion.4
  79.8 0.9 copy.16
  80.7 0.0 reduce-scatter.4.cloned.1.call-update
  80.7 22.9 %reduce-scatter.4.cloned.1.call-done = bf16[64,576]{1,0:T(8,128)(2,1)} async-done(((bf16[256,576]{1,0:T(8,128)(2,1)}), bf16[64,576]{1,0:T(8,128)(2,1)}) %reduce-scatter.4.cloned.1.call-update) | async-done | bytes 73744 | tf_op jit(solution)/shard_map/reduce_scatter | solution.py:63
  103.6 9.2 %all_gather.23 = bf16[256,576]{1,0:T(8,128)(2,1)S(1)} all-gather(bf16[64,576]{1,0:T(8,128)(2,1)} %reduce-scatter.4.cloned.1.call-done), channel_id=1, replica_groups=mesh['head'=4,'seq'=8] {'head'}, dimensions={0}, use_global_device_ids=true | all-gather | bytes 368640 | tf_op jit(solution)/shard_map/all_gather | solution.py:75
  112.8 1.0 copy.13
  113.7 0.0 copy-done
  113.7 1.8 %convolution_convert_fusion = bf16[256,1792]{1,0:T(8,128)(2,1)} fusion(bf16[256,576]{1,0:T(8,128)(2,1)S(1)} %all_gather.23, bf16[1792,576]{0,1:T(8,128)(2,1)S(1)} %copy-done), kind=kOutput, calls=%fused_computation.5 | convolution fusion | flops 528941056 | bytes 3276800 | tf_op jit(solution)/shard_map/dot_general | solution.py:78
  (16 shorter events, 0.2 us)
Async XLA Ops:
  7.2 106.6 %copy-start = (bf16[1792,576]{0,1:T(8,128)(2,1)S(1)}, bf16[1792,576]{0,1:T(8,128)(2,1)}, u32[]{:S(2)}) copy-start(bf16[1792,576]{0,1:T(8,128)(2,1)} %param.13) | copy-start | bytes 6193156
  8.7 22.8 %all-to-all-start = ((bf16[8,1,16,576]{3,2,1,0:T(8,128)(2,1)}), bf16[8,1,16,576]{3,2,1,0:T(8,128)(2,1)S(1)}, u32[]{:S(2)}, u32[]{:S(2)}) async-start(bf16[8,1,16,576]{3,2,1,0:T(8,128)(2,1)} %stack.2), calls=%async_computation | async-start | bytes 327680 | tf_op jit(solution)/shard_map/all_to_all | solution.py:29
  15.1 88.5 %reduce-scatter.4.cloned.1.call-start = ((), (), s32[]{:S(2)}) async-start(), calls=%async_computation.2 | async-start | bytes 409600 | tf_op jit(solution)/shard_map/reduce_scatter | solution.py:63
Sparse Core Ops, SparseCore 0:
  80.8 22.6 reduce-scatter.3
